TPU v7x, 256 devices: a whole 4x4x8 slice. The times are simulated.
256 devices in a mesh: seq: 32 (over z_hi, x, core), head: 8 (over y, z_lo).
Axes of the slice: x: 4, y: 4, z: 8 (z_hi: 4, z_lo: 2; z = z_hi * 2 + z_lo), core: 2. Of those that a mesh axis runs over, the one named last changes fastest.
Arguments:
- queries: bfloat16 [6144, 4096], P('seq', 'head'), may hold values from -12.5 to 12.5
- keys: bfloat16 [6144, 1024], P('seq', 'head'), may hold values from -10.5 to 10.5
- values: bfloat16 [6144, 1024], P('seq', 'head'), may hold values from -6 to 6
- d_out: bfloat16 [6144, 4096], P('seq', 'head'), may hold values from -6 to 6
- w_out: bfloat16 [4096, 4096], P('head'), may hold values from -0.09375 to 0.09375
- doc_starts: int32 [4], replicated, may hold values from 0 to 6128, as said below
Outputs:
- query_grad: bfloat16 [6144, 4096], P('seq', 'head')
- key_grad: bfloat16 [6144, 1024], P('seq', 'head')
- value_grad: bfloat16 [6144, 1024], P('seq', 'head')
Inputs may be any that keep to these rules, and one draw needn't show every extreme that they name: doc_starts[0] is 0, the entries rise strictly, every entry is a multiple of 16, and the last entry is 6128, so the last document has 16 positions; a document runs from its start to the next start or to the end of the sequence.
All inputs are finite; a program needn't handle non-finite values.
Results may differ from a plain program's by a relative error of at most 0.0163.
Values may be sent and summed in bfloat16 or wider, within the bound.
A program may use at most 128 MiB of HBM per device.

v0:
```python
import math
import jax
import jax.numpy as jnp
from jax import lax
from jax.sharding import PartitionSpec as P

DH = 128
NEG_FILL = -1e30


def doc_index(doc_starts, places):
    return jnp.sum((places[:, None] >= doc_starts[None, :]).astype(jnp.int32), axis=1)


def allowed_pairs(doc_starts, row_ids, col_ids):
    earlier = col_ids[None, :] <= row_ids[:, None]
    same_doc = doc_index(doc_starts, row_ids)[:, None] == doc_index(doc_starts, col_ids)[None, :]
    return (earlier & same_doc)[None, None]


def softmax_grads(q_four, g_four, key_three, value_three, allowed, log_total, row_delta, scaling):
    scores = (
        jnp.einsum("sghd,kgd->ghsk", q_four, key_three, preferred_element_type=jnp.float32)
        * scaling
    )
    prob_full = jnp.where(allowed, jnp.exp(scores - log_total[..., None]), 0.0)
    grad_dots = jnp.einsum(
        "sghd,kgd->ghsk", g_four, value_three, preferred_element_type=jnp.float32
    )
    dscores = prob_full * (grad_dots - row_delta[..., None]) * scaling
    return (prob_full.astype(jnp.bfloat16), dscores.astype(jnp.bfloat16))


def shards(queries, keys, values, d_out, w_out, doc_starts):
    rows_here = queries.shape[0]
    head_size = DH
    groups = keys.shape[1] // head_size
    per_group = queries.shape[1] // keys.shape[1]
    scaling = 1.0 / math.sqrt(head_size)
    first_row = lax.axis_index("seq") * rows_here
    my_rows = first_row + jnp.arange(rows_here, dtype=jnp.int32)
    weights = w_out
    attn_grad = lax.dot_general(
        lax.all_gather(d_out, "head", axis=1, tiled=True),
        weights,
        (((1,), (1,)), ((), ())),
        preferred_element_type=jnp.float32,
    )
    attn_grad = attn_grad.astype(jnp.bfloat16)
    query_four = queries.reshape(rows_here, groups, per_group, head_size)
    grad_four = attn_grad.reshape(rows_here, groups, per_group, head_size)
    stat_shape = (groups, per_group, rows_here)
    key_block = lax.all_gather(keys, "seq", axis=0, tiled=True)
    value_block = lax.all_gather(values, "seq", axis=0, tiled=True)
    piece_rows = key_block.shape[0]
    allowed = allowed_pairs(doc_starts, my_rows, jnp.arange(piece_rows, dtype=jnp.int32))
    key_three = key_block.reshape(piece_rows, groups, head_size)
    value_three = value_block.reshape(piece_rows, groups, head_size)
    scores = (
        jnp.einsum("sghd,kgd->ghsk", query_four, key_three, preferred_element_type=jnp.float32)
        * scaling
    )
    scores = jnp.where(allowed, scores, NEG_FILL)
    high_old = jnp.full(stat_shape, NEG_FILL, jnp.float32)
    high_new = jnp.maximum(high_old, jnp.max(scores, axis=-1))
    weights = jnp.where(allowed, jnp.exp(scores - high_new[..., None]), 0.0)
    grad_dots = jnp.einsum(
        "sghd,kgd->ghsk", grad_four, value_three, preferred_element_type=jnp.float32
    )
    total_new = jnp.sum(weights, axis=-1)
    accum_new = jnp.sum(weights * grad_dots, axis=-1)
    log_total = high_new + jnp.log(total_new)
    row_delta = accum_new / total_new
    key_block = lax.all_gather(keys, "seq", axis=0, tiled=True)
    value_block = lax.all_gather(values, "seq", axis=0, tiled=True)
    piece_rows = key_block.shape[0]
    allowed = allowed_pairs(doc_starts, my_rows, jnp.arange(piece_rows, dtype=jnp.int32))
    key_three = key_block.reshape(piece_rows, groups, head_size)
    value_three = value_block.reshape(piece_rows, groups, head_size)
    prob_half, dscores = softmax_grads(
        query_four, grad_four, key_three, value_three, allowed, log_total, row_delta, scaling
    )
    key_three, prob_half, dscores, piece_rows = (key_three, prob_half, dscores, piece_rows)
    query_acc = jnp.einsum("ghsk,kgd->sghd", dscores, key_three, preferred_element_type=jnp.float32)
    key_piece = jnp.einsum(
        "ghsk,sghd->kgd", dscores, query_four, preferred_element_type=jnp.float32
    )
    value_piece = jnp.einsum(
        "ghsk,sghd->kgd", prob_half, grad_four, preferred_element_type=jnp.float32
    )
    key_acc = key_piece
    value_acc = value_piece
    query_acc, key_terms, value_terms = (query_acc, key_acc, value_acc)
    key_acc, value_acc = (
        lax.psum_scatter(
            key_terms.astype(jnp.bfloat16), "seq", scatter_dimension=0, tiled=True
        ).astype(jnp.float32),
        lax.psum_scatter(
            value_terms.astype(jnp.bfloat16), "seq", scatter_dimension=0, tiled=True
        ).astype(jnp.float32),
    )
    query_grad = query_acc.reshape(rows_here, groups * per_group * head_size).astype(jnp.bfloat16)
    key_grad = key_acc.reshape(rows_here, groups * head_size).astype(jnp.bfloat16)
    value_grad = value_acc.reshape(rows_here, groups * head_size).astype(jnp.bfloat16)
    return (query_grad, key_grad, value_grad)


def solution(mesh):
    return jax.shard_map(
        shards,
        mesh=mesh,
        in_specs=(
            P("seq", "head"),
            P("seq", "head"),
            P("seq", "head"),
            P("seq", "head"),
            P("head", None),
            P(),
        ),
        out_specs=(P("seq", "head"), P("seq", "head"), P("seq", "head")),
        check_vma=False,
    )
```

profile of v0, /device:TPU:8, one launch (start us, length us, event | category | flops | bytes accessed | tf_op | source)
XLA Modules:
  0.0 378.5 jit_solution(6322208966597983329)
XLA Ops:
  7.2 0.0 copy-start
  7.2 0.0 all-gather.6.cloned.1.call-start
  7.2 0.7 all-gather.6.cloned.1.call-update
  7.9 0.0 all-gather.4.cloned.1.call-start
  8.0 0.7 all-gather.4.cloned.1.call-update
  8.7 0.0 all-gather.8.cloned.1.call-start
  8.7 0.7 all-gather.8.cloned.1.call-update
  9.4 0.0 reduce-scatter.7.cloned.1.call-start
  9.5 0.7 convert_reduce_fusion.1
  10.2 0.8 convert_reduce_fusion
  11.0 1.0 fusion.25
  12.0 45.0 %all-gather.6.cloned.1.call-done = bf16[192,4096]{1,0:T(8,128)(2,1)} async-done(((bf16[192,512]{1,0:T(8,128)(2,1)}), bf16[192,4096]{1,0:T(8,128)(2,1)}) %all-gather.6.cloned.1.call-update) | async-done | bytes 1572880 | tf_op jit(solution)/shard_map/all_gather | solution.py:44
  57.0 4.2 %fusion.38 = bf16[24,4,8,128]{3,2,1,0:T(8,128)(2,1)S(1)} fusion(bf16[192,4096]{1,0:T(8,128)(2,1)} %all-gather.6.cloned.1.call-done, bf16[512,4096]{1,0:T(8,128)(2,1)} %param.10), kind=kOutput, calls=%fused_computation.35 | convolution fusion | flops 805404672 | bytes 5963776 | tf_op jit(solution)/shard_map/dot_general | solution.py:43
  61.2 52.1 %all-gather.4.cloned.1.call-done = bf16[6144,128]{1,0:T(8,128)(2,1)} async-done(((bf16[192,128]{1,0:T(8,128)(2,1)}), bf16[6144,128]{1,0:T(8,128)(2,1)}) %all-gather.4.cloned.1.call-update) | async-done | bytes 1572880 | tf_op jit(solution)/shard_map/all_gather | solution.py:74
  113.3 0.0 copy-done
  113.3 9.9 %fusion.6 = (f32[4,192]{1,0:T(4,128)S(1)}, f32[6144,192,4]{0,1,2:T(8,128)}) fusion(pred[192,6144]{1,0:T(8,128)(4,1)S(1)} %fusion.25, bf16[6144,128]{1,0:T(8,128)(2,1)} %all-gather.4.cloned.1.call-done, bf16[192,512]{1,0:T(8,128)(2,1)S(1)} %copy-done), kind=kOutput, calls=%fused_computation.11 | convolution fusion | flops 1222114560 | bytes 21826560 | tf_op jit(solution)/shard_map/sghd,kgd->ghsk/dot_general | solution.py:23
  123.2 43.0 %all-gather.8.cloned.1.call-done = bf16[6144,128]{1,0:T(8,128)(2,1)} async-done(((bf16[192,128]{1,0:T(8,128)(2,1)}), bf16[6144,128]{1,0:T(8,128)(2,1)}) %all-gather.8.cloned.1.call-update) | async-done | bytes 1572880 | tf_op jit(solution)/shard_map/all_gather | solution.py:75
  166.2 15.5 %fusion.8 = (f32[4,192]{1,0:T(4,128)S(1)}, f32[4,192]{1,0:T(4,128)S(1)}, f32[192,4,6144]{2,0,1:T(8,128)}) fusion(f32[6144,192,4]{0,1,2:T(8,128)} %get-tuple-element.20, f32[4,192]{1,0:T(4,128)S(1)} %broadcast_maximum_fusion, pred[192,6144]{1,0:T(8,128)(4,1)S(1)} %fusion.25, bf16[6144,128]{1,0:T(8,128)(2,1)} %all-gather.8.cloned.1.call-done, ...), kind=kOutput, calls=%fused_computation.13 | convolution fusion | flops 1240988160 | bytes 40707072 | tf_op jit(solution)/shard_map/sghd,kgd->ghsk/dot_general | solution.py:27
  181.8 9.1 %fusion.21 = bf16[6144,128]{0,1:T(8,128)(2,1)S(1)} fusion(f32[6144,192,4]{0,1,2:T(8,128)} %get-tuple-element.20, f32[4,192]{1,0:T(4,128)S(1)} %get-tuple-element.17, pred[192,6144]{1,0:T(8,128)(4,1)S(1)} %fusion.25, bf16[24,4,8,128]{3,2,1,0:T(8,128)(2,1)S(1)} %fusion.38), kind=kOutput, calls=%fused_computation.22 | convolution fusion | flops 1227620352 | bytes 21826560 | tf_op jit(solution)/shard_map/ghsk,sghd->kgd/dot_general | solution.py:88
  190.8 1.6 copy.34
  192.4 0.0 reduce-scatter.7.cloned.1.call-update
  192.5 0.2 reduce-scatter.5.cloned.1.call-start
  192.7 13.7 %fusion.10 = bf16[4,192,6144]{2,1,0:T(8,128)(2,1)S(1)} fusion(f32[192,4,6144]{2,0,1:T(8,128)} %get-tuple-element.21, f32[6144,192,4]{0,1,2:T(8,128)} %get-tuple-element.20, f32[4,192]{1,0:T(4,128)S(1)} %get-tuple-element.18, f32[4,192]{1,0:T(4,128)S(1)} %get-tuple-element.17, pred[192,6144]{1,0:T(8,128)(4,1)S(1)} %fusion.25), kind=kLoop, calls=%fused_computation.15 | loop fusion | flops 33030144 | bytes 48371712 | tf_op jit(solution)/shard_map/reshape.24
  206.4 0.0 copy-start.1
  206.4 3.6 copy-done.1
  210.0 0.0 copy-start.2
  210.0 3.9 %fusion.24 = bf16[6144,1,128]{2,0,1:T(8,128)(2,1)} fusion(bf16[4,192,6144]{2,1,0:T(8,128)(2,1)S(1)} %fusion.10, bf16[192,512]{1,0:T(8,128)(2,1)S(1)} %copy-done), kind=kOutput, calls=%fused_computation.23 | convolution fusion | flops 1208745984 | bytes 11206656 | tf_op jit(solution)/shard_map/ghsk,sghd->kgd/dot_general | solution.py:85
  213.9 0.0 reduce-scatter.5.cloned.1.call-update
  213.9 0.0 copy-done.2
  213.9 6.4 %fusion.35 = bf16[192,1,4,128]{3,0,2,1:T(8,128)(2,1)S(1)} fusion(bf16[4,192,6144]{2,1,0:T(8,128)(2,1)} %copy-done.1, bf16[6144,128]{1,0:T(8,128)(2,1)S(1)} %copy-done.2), kind=kOutput, calls=%fused_computation.34 | convolution fusion | flops 1208057856 | bytes 11206656 | tf_op jit(solution)/shard_map/ghsk,kgd->sghd/dot_general | solution.py:84
  220.3 0.2 copy.28
  220.5 0.7 copy.60
  221.2 58.7 %reduce-scatter.7.cloned.1.call-done = bf16[192,128]{1,0:T(8,128)(2,1)} async-done(((bf16[6144,128]{1,0:T(8,128)(2,1)}), bf16[192,128]{1,0:T(8,128)(2,1)}) %reduce-scatter.7.cloned.1.call-update) | async-done | bytes 49168
  279.9 92.1 %reduce-scatter.5.cloned.1.call-done = bf16[192,1,128]{2,0,1:T(8,128)(2,1)} async-done(((bf16[6144,1,128]{2,0,1:T(8,128)(2,1)}), bf16[192,1,128]{2,0,1:T(8,128)(2,1)}) %reduce-scatter.5.cloned.1.call-update) | async-done | bytes 49168 | tf_op jit(solution)/shard_map/reduce_scatter | solution.py:95
  (3 shorter events, 0.0 us)
Async XLA Ops:
  7.2 106.2 %copy-start = (bf16[192,512]{1,0:T(8,128)(2,1)S(1)}, bf16[192,512]{1,0:T(8,128)(2,1)}, u32[]{:S(2)}) copy-start(bf16[192,512]{1,0:T(8,128)(2,1)} %param.6) | copy-start | bytes 589828
  7.2 49.8 %all-gather.6.cloned.1.call-start = ((), (), s32[]{:S(2)}) async-start(), calls=%async_computation.3 | async-start | bytes 1769472 | tf_op jit(solution)/shard_map/all_gather | solution.py:44
  7.9 105.4 %all-gather.4.cloned.1.call-start = ((), (), s32[]{:S(2)}) async-start(), calls=%async_computation.2 | async-start | bytes 1622016 | tf_op jit(solution)/shard_map/all_gather | solution.py:74
  8.7 157.5 %all-gather.8.cloned.1.call-start = ((), (), s32[]{:S(2)}) async-start(), calls=%async_computation.4 | async-start | bytes 1622016 | tf_op jit(solution)/shard_map/all_gather | solution.py:75
  9.4 270.5 %reduce-scatter.7.cloned.1.call-start = ((), (), s32[]{:S(2)}) async-start(), calls=%async_computation.6 | async-start | bytes 1622016
  192.5 179.5 %reduce-scatter.5.cloned.1.call-start = ((), (), s32[]{:S(2)}) async-start(), calls=%async_computation.5 | async-start | bytes 1622016 | tf_op jit(solution)/shard_map/reduce_scatter | solution.py:95
  206.4 3.6 copy-start.1
  210.0 3.9 %copy-start.2 = (bf16[6144,128]{1,0:T(8,128)(2,1)S(1)}, bf16[6144,128]{1,0:T(8,128)(2,1)}, u32[]{:S(2)}) copy-start(bf16[6144,128]{1,0:T(8,128)(2,1)} %all-gather.4.cloned.1.call-done) | copy-start | bytes 4718596
Sparse Core Ops, SparseCore 0:
  9.8 47.1 all-gather.5
  59.5 53.7 all-gather.3
  115.9 50.2 all-gather.7
  192.6 87.3 reduce-scatter.6
  284.2 87.7 reduce-scatter.4
where the time goes:
time: 379 us
  waiting for transfers between devices  293 us (77%)
  matrix products  49 us (13%)
  other arithmetic  16.2 us (4%)
  between operations  13.9 us (4%)
  local copies, waits for them, and re-layouts  6.1 us (2%)
    reduce_scatter x1, waiting for transfers between devices, shards(): lax.psum_scatter(key_terms.astype(jnp.bfloat16), 'seq', scatter_dimension...  92.1 us
    unnamed x6, waiting for transfers between devices  60.8 us
    all_gather x1, waiting for transfers between devices, shards(): key_block = lax.all_gather(keys, 'seq', axis=0, tiled=True)  52.1 us
    all_gather x1, waiting for transfers between devices, shards(): lax.all_gather(d_out, 'head', axis=1, tiled=True)  45 us
    all_gather x1, waiting for transfers between devices, shards(): value_block = lax.all_gather(values, 'seq', axis=0, tiled=True)  43 us
    dot_general x1, matrix products, softmax_grads(): jnp.einsum('sghd,kgd->ghsk', g_four, value_three, preferred_element_type=...  15.5 us
    another operation x1, other arithmetic  13.7 us
    dot_general x1, matrix products, softmax_grads(): jnp.einsum('sghd,kgd->ghsk', q_four, key_three, preferred_element_type=jn...  9.9 us
  transfers between devices with their start and end apart: 5, of which 5 were waited for; matrix products, arithmetic and copies ran while one was open for 11% of the time, Pallas kernels for 0%

commit v1 on v0

--- a/solution.py
+++ b/solution.py
@@ -71,8 +71,11 @@
     accum_new = jnp.sum(weights * grad_dots, axis=-1)
     log_total = high_new + jnp.log(total_new)
     row_delta = accum_new / total_new
-    key_block = lax.all_gather(keys, "seq", axis=0, tiled=True)
-    value_block = lax.all_gather(values, "seq", axis=0, tiled=True)
+    key_block, value_block = jnp.split(
+        lax.all_gather(jnp.concatenate([keys, values], axis=1), "seq", axis=0, tiled=True),
+        [keys.shape[1]],
+        axis=1,
+    )
     piece_rows = key_block.shape[0]
     allowed = allowed_pairs(doc_starts, my_rows, jnp.arange(piece_rows, dtype=jnp.int32))
     key_three = key_block.reshape(piece_rows, groups, head_size)

time: 379 us -> 433 us (1.14)
  waiting for transfers between devices: 293 us -> 332 us
  matrix products: 49 us -> 62.2 us
  local copies, waits for them, and re-layouts: 6.1 us -> 13.5 us
  other arithmetic: 16.2 us -> 10.5 us
    all_gather x0 -> x1, waiting for transfers between devices: none -> 45.6 us  [shards(): lax.all_gather(jnp.concatenate([keys, values], axis=1), 'seq', axis=0, ti...]
    dot_general x0 -> x2, matrix products: none -> 16.7 us  [the longest x1 11.4 us: shards(): jnp.einsum('sghd,kgd->ghsk', grad_four, value_three, preferred_element_ty...]
    another operation x1 -> x0, other arithmetic: 13.7 us -> none
    all_gather x1, waiting for transfers between devices: 43 us -> 34.7 us  [shards(): value_block = lax.all_gather(values, 'seq', axis=0, tiled=True)]
    unnamed x8, local copies, waits for them, and re-layouts: 5.95 us -> 13.4 us
    reduce_sum x0 -> x1, other arithmetic: none -> 6.46 us  [shards(): total_new = jnp.sum(weights, axis=-1)]
    dot_general x1, matrix products: 15.5 us -> 11 us  [softmax_grads(): jnp.einsum('sghd,kgd->ghsk', g_four, value_three, preferred_element_type=...]
    unnamed x6 -> x7, waiting for transfers between devices: 60.8 us -> 63.9 us
  transfers between devices with their start and end apart: 5 -> 6, of which waited for: 5 -> 6; matrix products, arithmetic and copies ran while one was open for 11% -> 12% of each run, Pallas kernels for 0% -> 0%
where the time goes in v1:
time: 433 us; the launch traced here: 432 us
  waiting for transfers between devices  332 us (77%)
  matrix products  62.2 us (14%)
  between operations  14.2 us (3%)
  local copies, waits for them, and re-layouts  13.5 us (3%)
  other arithmetic  10.5 us (2%)
    reduce_scatter x1, waiting for transfers between devices, shards(): lax.psum_scatter(key_terms.astype(jnp.bfloat16), 'seq', scatter_dimension...  92 us
    unnamed x7, waiting for transfers between devices  63.9 us
    all_gather x1, waiting for transfers between devices, shards(): key_block = lax.all_gather(keys, 'seq', axis=0, tiled=True)  52.1 us
    all_gather x1, waiting for transfers between devices, shards(): lax.all_gather(jnp.concatenate([keys, values], axis=1), 'seq', axis=0, ti...  45.6 us
    all_gather x1, waiting for transfers between devices, shards(): lax.all_gather(d_out, 'head', axis=1, tiled=True)  43.4 us
    all_gather x1, waiting for transfers between devices, shards(): value_block = lax.all_gather(values, 'seq', axis=0, tiled=True)  34.7 us
    unnamed x8, local copies, waits for them, and re-layouts  13.4 us
    dot_general x1, matrix products, shards(): jnp.einsum('sghd,kgd->ghsk', grad_four, value_three, preferred_element_ty...  11.4 us
  transfers between devices with their start and end apart: 6, of which 6 were waited for; matrix products, arithmetic and copies ran while one was open for 12% of the time, Pallas kernels for 0%

profile of v1, /device:TPU:8, one launch (start us, length us, event | category | flops | bytes accessed | tf_op | source)
XLA Modules:
  0.0 432.5 jit_solution(7986096271883160714)
XLA Ops:
  7.2 0.0 copy-start
  7.2 0.0 all-gather.9.cloned.1.call-start
  7.2 0.7 all-gather.9.cloned.1.call-update
  7.9 0.0 all-gather.7.cloned.1.call-start
  8.0 0.7 all-gather.7.cloned.1.call-update
  8.7 0.0 all-gather.11.cloned.1.call-start
  8.7 0.7 all-gather.11.cloned.1.call-update
  9.4 0.0 all-gather.5.cloned.1.call-start
  9.4 1.5 pad_maximum_fusion
  10.9 0.0 all-gather.5.cloned.1.call-update
  10.9 0.0 reduce-scatter.7.cloned.1.call-start
  11.0 0.8 convert_reduce_fusion
  11.8 0.7 convert_reduce_fusion.1
  12.5 1.0 fusion.35
  13.6 43.4 %all-gather.9.cloned.1.call-done = bf16[192,4096]{1,0:T(8,128)(2,1)} async-done(((bf16[192,512]{1,0:T(8,128)(2,1)}), bf16[192,4096]{1,0:T(8,128)(2,1)}) %all-gather.9.cloned.1.call-update) | async-done | bytes 1572880 | tf_op jit(solution)/shard_map/all_gather | solution.py:44
  57.0 4.2 fusion.46
  61.2 52.1 %all-gather.7.cloned.1.call-done = bf16[6144,128]{1,0:T(8,128)(2,1)} async-done(((bf16[192,128]{1,0:T(8,128)(2,1)}), bf16[6144,128]{1,0:T(8,128)(2,1)}) %all-gather.7.cloned.1.call-update) | async-done | bytes 1572880 | tf_op jit(solution)/shard_map/all_gather | solution.py:53
  113.3 0.0 copy-done
  113.3 5.3 %fusion.6 = (f32[4,192]{1,0:T(4,128)S(1)}, f32[6144,192,4]{0,1,2:T(8,128)S(1)}) fusion(pred[192,6144]{1,0:T(8,128)(4,1)S(1)} %fusion.35, bf16[6144,128]{1,0:T(8,128)(2,1)} %all-gather.7.cloned.1.call-done, bf16[192,512]{1,0:T(8,128)(2,1)S(1)} %copy-done), kind=kOutput, calls=%fused_computation.11 | convolution fusion | flops 1222114560 | bytes 21826560 | tf_op jit(solution)/shard_map/sghd,kgd->ghsk/dot_general | solution.py:60
  118.6 0.0 copy-start.1
  118.6 6.4 %copy-done.1 = f32[6144,192,4]{0,1,2:T(8,128)} copy-done((f32[6144,192,4]{0,1,2:T(8,128)}, f32[6144,192,4]{0,1,2:T(8,128)S(1)}, u32[]{:S(2)}) %copy-start.1) | copy-done | bytes 18874392
  125.1 6.5 %fusion.8 = f32[4,192]{1,0:T(4,128)S(1)} fusion(f32[6144,192,4]{0,1,2:T(8,128)S(1)} %get-tuple-element.18, f32[4,192]{1,0:T(4,128)S(1)} %broadcast_maximum_fusion, pred[192,6144]{1,0:T(8,128)(4,1)S(1)} %fusion.35), kind=kLoop, calls=%fused_computation.13 | loop fusion | flops 23592192 | bytes 20060160 | tf_op jit(solution)/shard_map/reduce_sum | solution.py:70
  131.5 34.7 %all-gather.11.cloned.1.call-done = bf16[6144,128]{1,0:T(8,128)(2,1)} async-done(((bf16[192,128]{1,0:T(8,128)(2,1)}), bf16[6144,128]{1,0:T(8,128)(2,1)}) %all-gather.11.cloned.1.call-update) | async-done | bytes 1572880 | tf_op jit(solution)/shard_map/all_gather | solution.py:54
  166.2 11.4 %fusion = f32[4,192]{1,0:T(4,128)S(1)} fusion(f32[6144,192,4]{0,1,2:T(8,128)} %copy-done.1, f32[4,192]{1,0:T(4,128)S(1)} %broadcast_maximum_fusion, pred[192,6144]{1,0:T(8,128)(4,1)S(1)} %fusion.35, bf16[6144,128]{1,0:T(8,128)(2,1)} %all-gather.11.cloned.1.call-done, bf16[24,4,8,128]{3,2,1,0:T(8,128)(2,1)S(1)} %fusion.46), kind=kOutput, calls=%fused_computation.1 | convolution fusion | flops 1236270336 | bytes 21829632 | tf_op jit(solution)/shard_map/sghd,kgd->ghsk/dot_general | solution.py:67
  177.7 45.6 %all-gather.5.cloned.1.call-done = bf16[6144,256]{1,0:T(8,128)(2,1)} async-done(((bf16[192,256]{1,0:T(8,128)(2,1)}), bf16[6144,256]{1,0:T(8,128)(2,1)}) %all-gather.5.cloned.1.call-update) | async-done | bytes 3145744 | tf_op jit(solution)/shard_map/all_gather | solution.py:75
  223.3 9.3 %fusion.39 = f32[6144,192,4]{0,1,2:T(8,128)} fusion(bf16[6144,256]{1,0:T(8,128)(2,1)} %all-gather.5.cloned.1.call-done, bf16[192,512]{1,0:T(8,128)(2,1)S(1)} %copy-done), kind=kOutput, calls=%fused_computation.34 | convolution fusion | flops 1207959552 | bytes 20643840 | tf_op jit(solution)/shard_map/sghd,kgd->ghsk/dot_general | solution.py:23
  232.6 10.2 %fusion.29 = bf16[6144,128]{0,1:T(8,128)(2,1)} fusion(f32[6144,192,4]{0,1,2:T(8,128)} %fusion.39, f32[4,192]{1,0:T(4,128)S(1)} %get-tuple-element.15, pred[192,6144]{1,0:T(8,128)(4,1)S(1)} %fusion.35, bf16[24,4,8,128]{3,2,1,0:T(8,128)(2,1)S(1)} %fusion.46), kind=kOutput, calls=%fused_computation.25 | convolution fusion | flops 1227620352 | bytes 21826560 | tf_op jit(solution)/shard_map/ghsk,sghd->kgd/dot_general | solution.py:91
  242.8 2.6 copy.42
  245.4 0.0 reduce-scatter.7.cloned.1.call-update
  245.5 0.0 reduce-scatter.5.cloned.1.call-start
  245.5 11.0 %fusion.3 = bf16[1,4,192,6144]{3,2,1,0:T(8,128)(2,1)S(1)} fusion(f32[6144,192,4]{0,1,2:T(8,128)} %fusion.39, f32[4,192]{1,0:T(4,128)S(1)} %get-tuple-element.16, f32[4,192]{1,0:T(4,128)S(1)} %get-tuple-element.15, pred[192,6144]{1,0:T(8,128)(4,1)S(1)} %fusion.35, bf16[6144,256]{1,0:T(8,128)(2,1)} %all-gather.5.cloned.1.call-done, ...), kind=kOutput, calls=%fused_computation.5 | convolution fusion | flops 1240989696 | bytes 31266816 | tf_op jit(solution)/shard_map/sghd,kgd->ghsk/dot_general | solution.py:27
  256.5 0.0 copy-start.2
  256.5 3.6 copy-done.2
  260.2 3.9 fusion.32
  264.0 0.0 reduce-scatter.5.cloned.1.call-update
  264.0 6.9 %fusion.43 = bf16[192,1,4,128]{3,0,2,1:T(8,128)(2,1)S(1)} fusion(bf16[1,4,192,6144]{3,2,1,0:T(8,128)(2,1)} %copy-done.2, bf16[6144,256]{1,0:T(8,128)(2,1)} %all-gather.5.cloned.1.call-done), kind=kOutput, calls=%fused_computation.37 | convolution fusion | flops 1208057856 | bytes 11206656 | tf_op jit(solution)/shard_map/ghsk,kgd->sghd/dot_general | solution.py:87
  271.0 0.2 copy.36
  271.1 0.7 copy.74
  271.8 61.7 %reduce-scatter.7.cloned.1.call-done = bf16[192,128]{1,0:T(8,128)(2,1)} async-done(((bf16[6144,128]{1,0:T(8,128)(2,1)}), bf16[192,128]{1,0:T(8,128)(2,1)}) %reduce-scatter.7.cloned.1.call-update) | async-done | bytes 49168
  333.6 92.0 %reduce-scatter.5.cloned.1.call-done = bf16[192,1,128]{2,0,1:T(8,128)(2,1)} async-done(((bf16[6144,1,128]{2,0,1:T(8,128)(2,1)}), bf16[192,1,128]{2,0,1:T(8,128)(2,1)}) %reduce-scatter.5.cloned.1.call-update) | async-done | bytes 49168 | tf_op jit(solution)/shard_map/reduce_scatter | solution.py:98
  (3 shorter events, 0.0 us)
Async XLA Ops:
  7.2 106.2 %copy-start = (bf16[192,512]{1,0:T(8,128)(2,1)S(1)}, bf16[192,512]{1,0:T(8,128)(2,1)}, u32[]{:S(2)}) copy-start(bf16[192,512]{1,0:T(8,128)(2,1)} %param.6) | copy-start | bytes 589828
  7.2 49.8 %all-gather.9.cloned.1.call-start = ((), (), s32[]{:S(2)}) async-start(), calls=%async_computation.4 | async-start | bytes 1769472 | tf_op jit(solution)/shard_map/all_gather | solution.py:44
  7.9 105.4 %all-gather.7.cloned.1.call-start = ((), (), s32[]{:S(2)}) async-start(), calls=%async_computation.3 | async-start | bytes 1622016 | tf_op jit(solution)/shard_map/all_gather | solution.py:53
  8.7 157.5 %all-gather.11.cloned.1.call-start = ((), (), s32[]{:S(2)}) async-start(), calls=%async_computation.5 | async-start | bytes 1622016 | tf_op jit(solution)/shard_map/all_gather | solution.py:54
  9.4 213.9 %all-gather.5.cloned.1.call-start = ((), (), s32[]{:S(2)}) async-start(), calls=%async_computation.2 | async-start | bytes 3244032 | tf_op jit(solution)/shard_map/all_gather | solution.py:75
  10.9 322.6 %reduce-scatter.7.cloned.1.call-start = ((), (), s32[]{:S(2)}) async-start(), calls=%async_computation.7 | async-start | bytes 1622016
  118.6 6.5 %copy-start.1 = (f32[6144,192,4]{0,1,2:T(8,128)}, f32[6144,192,4]{0,1,2:T(8,128)S(1)}, u32[]{:S(2)}) copy-start(f32[6144,192,4]{0,1,2:T(8,128)S(1)} %get-tuple-element.18) | copy-start | bytes 56623108
  245.5 180.1 %reduce-scatter.5.cloned.1.call-start = ((), (), s32[]{:S(2)}) async-start(), calls=%async_computation.6 | async-start | bytes 1622016 | tf_op jit(solution)/shard_map/reduce_scatter | solution.py:98
  256.5 3.6 copy-start.2
Sparse Core Ops, SparseCore 0:
  9.8 47.1 all-gather.8
  59.5 53.7 all-gather.6
  115.9 50.2 all-gather.10
  169.2 54.0 all-gather.4
  245.6 87.9 reduce-scatter.6
  337.8 87.7 reduce-scatter.4
